TPU v7x, 32 devices: a whole 2x2x4 slice. The times are simulated.
32 devices in a mesh: ctx: 8 (over z, x), tp: 4 (over y, core).
Axes of the slice: x: 2, y: 2, z: 4, core: 2. Of those that a mesh axis runs over, the one named last changes fastest.
Arguments:
- inputs: bfloat16 [4096, 768], P(('ctx', 'tp')), may hold values from -6 to 6
- positions: int32 [4096], P('ctx'), may hold values from 0 to 3071, as said below
- attn_scale: float32 [768], replicated, may hold values from 0.1 to 1.9
- attn_shift: float32 [768], replicated, may hold values from -4 to 4
- mlp_scale: float32 [768], replicated, may hold values from 0.1 to 1.9
- mlp_shift: float32 [768], replicated, may hold values from -4 to 4
- qkv_weight: bfloat16 [768, 3, 768], P(None, None, 'tp'), may hold values from -0.21875 to 0.21875
- qv_bias: float32 [2, 768], P(None, 'tp'), may hold values from -4 to 4
- dense_weight: bfloat16 [768, 768], P('tp'), may hold values from -1.75 to 1.75
- dense_bias: float32 [768], replicated, may hold values from -5 to 5
- up_weight: bfloat16 [768, 3072], P(None, 'tp'), may hold values from -0.21875 to 0.21875
- up_bias: float32 [3072], P('tp'), may hold values from -4 to 4
- down_weight: bfloat16 [3072, 768], P('tp'), may hold values from -0.109375 to 0.109375
- down_bias: float32 [768], replicated, may hold values from -5 to 5
- cotangent: bfloat16 [4096, 768], P(('ctx', 'tp')), may hold values from -6 to 6
Outputs:
- output: bfloat16 [4096, 768], P(('ctx', 'tp'))
- grad_input: float32 [4096, 768], P(('ctx', 'tp'))
- grad_attn_scale: float32 [768], replicated
- grad_attn_shift: float32 [768], replicated
- grad_mlp_scale: float32 [768], replicated
- grad_mlp_shift: float32 [768], replicated
- grad_qkv: float32 [768, 3, 768], P(None, None, 'tp')
- grad_qv_bias: float32 [2, 768], P(None, 'tp')
- grad_dense: float32 [768, 768], P('tp')
- grad_dense_bias: float32 [768], replicated
- grad_up: float32 [768, 3072], P(None, 'tp')
- grad_up_bias: float32 [3072], P('tp')
- grad_down: float32 [3072, 768], P('tp')
- grad_down_bias: float32 [768], replicated
Inputs may be any that keep to these rules, and one draw needn't show every extreme that they name: The sequence holds three documents; positions count from 0 at each document's first token and rise by one along it; the second document has 3072 tokens and starts at a token between 1 and 1023.
All inputs are finite; a program needn't handle non-finite values.
Results may differ from a plain program's by a relative error of at most 0.025.
Values may be sent and summed in bfloat16 or wider, within the bound.
A program may use at most 128 MiB of HBM per device.

v0:
```python
import math
import jax
import jax.numpy as jnp
from jax import lax
from jax.sharding import PartitionSpec as P

D = 768
HD = 64
ROT = 16
norm_eps = 1e-05


def layer_norm(values, scale, shift):
    mean_value = jnp.mean(values, axis=-1, keepdims=True)
    centred = values - mean_value
    variance = jnp.mean(centred * centred, axis=-1, keepdims=True)
    inv_std = lax.rsqrt(variance + norm_eps)
    normal_part = centred * inv_std
    return (normal_part * scale + shift, normal_part, inv_std)


def norm_backward(grad_normed, normal_part, inv_std, scale):
    grad_hat = grad_normed * scale
    mean_grad = jnp.mean(grad_hat, axis=-1, keepdims=True)
    mean_mixed = jnp.mean(grad_hat * normal_part, axis=-1, keepdims=True)
    return inv_std * (grad_hat - mean_grad - normal_part * mean_mixed)


def rotary_tables(positions):
    freqs = 10000.0 ** (-jnp.arange(0, ROT, 2).astype(jnp.float32) / ROT)
    angles = positions.astype(jnp.float32)[:, None] * freqs[None, :]
    angles = jnp.concatenate([angles, angles], axis=1)
    return (jnp.cos(angles), jnp.sin(angles))


def rotate(tensor, cosines, sines):
    part = tensor[..., :ROT]
    half = ROT // 2
    turned = jnp.concatenate([-part[..., half:], part[..., :half]], axis=-1)
    spun = part * cosines[:, None, :] + turned * sines[:, None, :]
    return jnp.concatenate([spun, tensor[..., ROT:]], axis=-1)


def gelu_grad(pre_act):
    cumulative = 0.5 * (1.0 + jax.scipy.special.erf(pre_act * 0.7071067811865476))
    density = jnp.exp(-0.5 * pre_act * pre_act) * 0.3989422804014327
    return cumulative + pre_act * density


def block_length(length):
    return math.gcd(length, 1024)


def local(
    inputs,
    positions,
    attn_scale,
    attn_shift,
    mlp_scale,
    mlp_shift,
    qkv_weight,
    qv_bias,
    dense_weight,
    dense_bias,
    up_weight,
    up_bias,
    down_weight,
    down_bias,
    cotangent,
):
    local_width = qkv_weight.shape[2]
    head_count = local_width // HD
    score_scale = HD ** (-0.5)
    resid = inputs.astype(jnp.float32)
    normed_one, hat_one, std_one = layer_norm(resid, attn_scale, attn_shift)
    normed_two, hat_two, std_two = layer_norm(resid, mlp_scale, mlp_shift)
    attn_in, mlp_in = (
        lax.all_gather(normed_one.astype(jnp.bfloat16), "tp", axis=0, tiled=True),
        lax.all_gather(normed_two.astype(jnp.bfloat16), "tp", axis=0, tiled=True),
    )
    block_rows = attn_in.shape[0]
    proj = jnp.dot(
        attn_in, qkv_weight.reshape(D, 3 * local_width), preferred_element_type=jnp.float32
    )
    proj = proj.reshape(block_rows, 3, head_count, HD)
    cosines, sines = rotary_tables(positions)
    queries = rotate(proj[:, 0] + qv_bias[0].reshape(head_count, HD), cosines, sines).astype(
        jnp.bfloat16
    )
    keys_rot = rotate(proj[:, 1], cosines, sines).astype(jnp.bfloat16)
    values = (proj[:, 2] + qv_bias[1].reshape(head_count, HD)).astype(jnp.bfloat16)
    own_start = lax.axis_index("ctx") * block_rows
    query_pos = own_start + jnp.arange(block_rows, dtype=jnp.int32)
    first_key = query_pos - positions
    last_query = query_pos[block_rows - 1]
    earliest_key = jnp.min(first_key)

    def visible_mask(start_row, length):
        key_pos = start_row + jnp.arange(length, dtype=jnp.int32)
        return (key_pos[None, :] <= query_pos[:, None]) & (key_pos[None, :] >= first_key[:, None])

    def reachable(start_row, length):
        return (start_row <= last_query) & (start_row + length - 1 >= earliest_key)

    def attend_block(running, key_block, value_block, start_row):
        row_max, row_sum, accumulated = running
        visible = visible_mask(start_row, key_block.shape[0])
        scores = (
            jnp.einsum("qhd,khd->hqk", queries, key_block, preferred_element_type=jnp.float32)
            * score_scale
        )
        scores = jnp.where(visible[None], scores, -1e30)
        new_max = jnp.maximum(row_max, jnp.max(scores, axis=-1))
        weights = jnp.where(visible[None], jnp.exp(scores - new_max[..., None]), 0.0)
        factor = jnp.exp(row_max - new_max)
        row_sum = row_sum * factor + jnp.sum(weights, axis=-1)
        accumulated = accumulated * factor[..., None] + jnp.einsum(
            "hqk,khd->hqd",
            weights.astype(jnp.bfloat16),
            value_block,
            preferred_element_type=jnp.float32,
        )
        return (new_max, row_sum, accumulated)

    initial = (
        jnp.full((head_count, block_rows), -1e30, jnp.float32),
        jnp.zeros((head_count, block_rows), jnp.float32),
        jnp.zeros((head_count, block_rows, HD), jnp.float32),
    )
    running = initial
    key_rows = lax.all_gather(keys_rot, "ctx", axis=0, tiled=True)
    value_rows = lax.all_gather(values, "ctx", axis=0, tiled=True)
    length = key_rows.shape[0]
    attend_step_rows = block_length(length)
    steps_count = length // attend_step_rows
    key_blocks = key_rows.reshape(steps_count, attend_step_rows, head_count, HD)
    value_blocks = value_rows.reshape(steps_count, attend_step_rows, head_count, HD)

    def one_step(current, inputs_step):
        key_block, value_block, number = inputs_step
        block_start = number * attend_step_rows

        def attend_now(state):
            return attend_block(state, key_block, value_block, block_start)

        def keep_state(state):
            return state

        return (
            lax.cond(reachable(block_start, attend_step_rows), attend_now, keep_state, current),
            None,
        )

    running, unused = lax.scan(
        one_step, running, (key_blocks, value_blocks, jnp.arange(steps_count, dtype=jnp.int32))
    )
    row_max, row_sum, accumulated = running
    attended = jnp.transpose(accumulated / row_sum[..., None], (1, 0, 2)).astype(jnp.bfloat16)
    log_total = row_max + jnp.log(row_sum)
    attended_flat = attended.reshape(block_rows, local_width)
    attn_part = jnp.dot(attended_flat, dense_weight, preferred_element_type=jnp.float32)
    pre_act = jnp.dot(mlp_in, up_weight, preferred_element_type=jnp.float32) + up_bias
    activation = jax.nn.gelu(pre_act, approximate=False).astype(jnp.bfloat16)
    mlp_part = jnp.dot(activation, down_weight, preferred_element_type=jnp.float32)
    branch_sum = lax.psum_scatter(attn_part + mlp_part, "tp", scatter_dimension=0, tiled=True)
    output = (resid + branch_sum + dense_bias + down_bias).astype(jnp.bfloat16)
    grad_out = cotangent.astype(jnp.float32)
    bias_grad = jnp.sum(grad_out, axis=0)
    grad_full = lax.all_gather(cotangent, "tp", axis=0, tiled=True)
    grad_down = jnp.dot(activation.T, grad_full, preferred_element_type=jnp.float32)
    grad_act = jnp.dot(grad_full, down_weight.T, preferred_element_type=jnp.float32)
    grad_pre = grad_act * gelu_grad(pre_act)
    grad_up_bias = jnp.sum(grad_pre, axis=0)
    grad_pre_low = grad_pre.astype(jnp.bfloat16)
    grad_up = jnp.dot(mlp_in.T, grad_pre_low, preferred_element_type=jnp.float32)
    grad_mlp_in = jnp.dot(grad_pre_low, up_weight.T, preferred_element_type=jnp.float32)
    grad_dense = jnp.dot(attended_flat.T, grad_full, preferred_element_type=jnp.float32)
    grad_attended = jnp.dot(grad_full, dense_weight.T, preferred_element_type=jnp.float32)
    grad_attended = grad_attended.astype(jnp.bfloat16).reshape(block_rows, head_count, HD)
    delta_rows = jnp.transpose(
        jnp.sum(grad_attended.astype(jnp.float32) * attended.astype(jnp.float32), axis=-1)
    )

    def score_grads(query_rows, grad_rows, log_rows, delta_part, key_block, value_block, visible):
        scores = (
            jnp.einsum("qhd,khd->hqk", query_rows, key_block, preferred_element_type=jnp.float32)
            * score_scale
        )
        weights = jnp.where(visible[None], jnp.exp(scores - log_rows[..., None]), 0.0)
        grad_weights = jnp.einsum(
            "qhd,khd->hqk", grad_rows, value_block, preferred_element_type=jnp.float32
        )
        grad_scores = (weights * (grad_weights - delta_part[..., None])).astype(jnp.bfloat16)
        return (weights.astype(jnp.bfloat16), grad_scores)

    key_back, value_back = (
        lax.all_gather(keys_rot, "ctx", axis=0, tiled=True),
        lax.all_gather(values, "ctx", axis=0, tiled=True),
    )
    total_rows = key_back.shape[0]
    step_rows = block_length(total_rows)
    steps_count = total_rows // step_rows
    back_inputs = (
        key_back.reshape(steps_count, step_rows, head_count, HD),
        value_back.reshape(steps_count, step_rows, head_count, HD),
        jnp.arange(steps_count, dtype=jnp.int32),
    )
    zero_query = jnp.zeros((block_rows, head_count, HD), jnp.float32)

    def back_step(query_grad, inputs_step):
        key_block, value_block, number = inputs_step
        block_start = number * step_rows

        def with_terms(grad_now):
            visible = visible_mask(block_start, step_rows)
            weights_low, grad_scores = score_grads(
                queries, grad_attended, log_total, delta_rows, key_block, value_block, visible
            )
            grad_now = (
                grad_now
                + jnp.einsum(
                    "hqk,khd->qhd", grad_scores, key_block, preferred_element_type=jnp.float32
                )
                * score_scale
            )
            key_part = (
                jnp.einsum("hqk,qhd->khd", grad_scores, queries, preferred_element_type=jnp.float32)
                * score_scale
            )
            value_part = jnp.einsum(
                "hqk,qhd->khd", weights_low, grad_attended, preferred_element_type=jnp.float32
            )
            joined = jnp.concatenate(
                [
                    key_part.reshape(step_rows, local_width),
                    value_part.reshape(step_rows, local_width),
                ],
                axis=1,
            )
            return (grad_now, joined)

        def without_terms(grad_now):
            return (grad_now, jnp.zeros((step_rows, 2 * local_width), jnp.float32))

        return lax.cond(reachable(block_start, step_rows), with_terms, without_terms, query_grad)

    query_grad, key_terms = lax.scan(back_step, zero_query, back_inputs)
    key_terms = key_terms.reshape(total_rows, 2 * local_width)
    own_terms = lax.psum_scatter(key_terms, "ctx", scatter_dimension=0, tiled=True)
    key_grad = own_terms[:, :local_width].reshape(block_rows, head_count, HD)
    value_grad = own_terms[:, local_width:].reshape(block_rows, head_count, HD)
    grad_query_pre = rotate(query_grad, cosines, -sines)
    grad_key_pre = rotate(key_grad, cosines, -sines)
    qv_bias_grad = jnp.stack(
        [
            jnp.sum(grad_query_pre, axis=0).reshape(local_width),
            jnp.sum(value_grad, axis=0).reshape(local_width),
        ]
    )
    grad_proj = jnp.stack([grad_query_pre, grad_key_pre, value_grad], axis=1)
    grad_proj = grad_proj.reshape(block_rows, 3 * local_width).astype(jnp.bfloat16)
    grad_qkv = jnp.dot(attn_in.T, grad_proj, preferred_element_type=jnp.float32).reshape(
        D, 3, local_width
    )
    grad_attn_in = jnp.dot(
        grad_proj, qkv_weight.reshape(D, 3 * local_width).T, preferred_element_type=jnp.float32
    )
    own_attn, own_mlp = (
        lax.psum_scatter(grad_attn_in, "tp", scatter_dimension=0, tiled=True),
        lax.psum_scatter(grad_mlp_in, "tp", scatter_dimension=0, tiled=True),
    )
    grad_input = grad_out + norm_backward(own_attn, hat_one, std_one, attn_scale)
    grad_input = grad_input + norm_backward(own_mlp, hat_two, std_two, mlp_scale)
    norm_sums = lax.psum(
        (
            jnp.sum(own_attn * hat_one, axis=0),
            jnp.sum(own_attn, axis=0),
            jnp.sum(own_mlp * hat_two, axis=0),
            jnp.sum(own_mlp, axis=0),
            bias_grad,
        ),
        ("ctx", "tp"),
    )
    weight_sums = lax.psum(
        (grad_qkv, qv_bias_grad, grad_dense, grad_up, grad_up_bias, grad_down), "ctx"
    )
    return (
        output,
        grad_input,
        norm_sums[0],
        norm_sums[1],
        norm_sums[2],
        norm_sums[3],
        weight_sums[0],
        weight_sums[1],
        weight_sums[2],
        norm_sums[4],
        weight_sums[3],
        weight_sums[4],
        weight_sums[5],
        norm_sums[4],
    )


def solution(mesh):
    in_specs = (
        P(("ctx", "tp"), None),
        P("ctx"),
        P(),
        P(),
        P(),
        P(),
        P(None, None, "tp"),
        P(None, "tp"),
        P("tp", None),
        P(),
        P(None, "tp"),
        P("tp"),
        P("tp", None),
        P(),
        P(("ctx", "tp"), None),
    )
    out_specs = (
        P(("ctx", "tp"), None),
        P(("ctx", "tp"), None),
        P(),
        P(),
        P(),
        P(),
        P(None, None, "tp"),
        P(None, "tp"),
        P("tp", None),
        P(),
        P(None, "tp"),
        P("tp"),
        P("tp", None),
        P(),
    )
    return jax.shard_map(local, mesh=mesh, in_specs=in_specs, out_specs=out_specs, check_vma=False)
```

profile of v0, /device:TPU:0, one launch (start us, length us, event | category | flops | bytes accessed | tf_op | source)
XLA Modules:
  0.0 690.6 jit_solution(9488253124478135631)
XLA Ops:
  11.5 10.1 %all_gather.17 = bf16[512,768]{1,0:T(8,128)(2,1)S(1)} all-gather(bf16[128,768]{1,0:T(8,128)(2,1)S(1)} %get-tuple-element.958), channel_id=1, replica_groups=mesh['ctx'=8,'tp'=4] {'tp'}, dimensions={0}, use_global_device_ids=true | all-gather | bytes 983040 | tf_op jit(solution)/shard_map/all_gather | solution.py:78
  27.7 8.7 %all_gather.21 = bf16[512,768]{1,0:T(8,128)(2,1)S(1)} all-gather(bf16[128,768]{1,0:T(8,128)(2,1)S(1)} %copy-done.29), channel_id=1, replica_groups=mesh['ctx'=8,'tp'=4] {'tp'}, dimensions={0}, use_global_device_ids=true | all-gather | bytes 983040 | tf_op jit(solution)/shard_map/all_gather | solution.py:169
  37.7 33.9 %all-gather.3.cloned.1.call-done = bf16[4096,3,64]{0,2,1:T(8,128)(2,1)} async-done(((bf16[512,3,64]{0,2,1:T(8,128)(2,1)}), bf16[4096,3,64]{0,2,1:T(8,128)(2,1)}) %all-gather.3.cloned.1.call-update) | async-done | bytes 1572880 | tf_op jit(solution)/shard_map/all_gather | solution.py:131
  73.2 43.7 %all-gather.5.cloned.1.call-done = bf16[4096,3,64]{0,2,1:T(8,128)(2,1)} async-done(((bf16[512,3,64]{0,2,1:T(8,128)(2,1)}), bf16[4096,3,64]{0,2,1:T(8,128)(2,1)}) %all-gather.5.cloned.1.call-update) | async-done | bytes 1572880 | tf_op jit(solution)/shard_map/all_gather | solution.py:132
  120.1 23.0 %while.39 = (s32[]{:T(128)}, f32[3,512]{1,0:T(4,128)S(1)}, f32[3,512]{1,0:T(4,128)S(1)}, f32[3,512,64]{1,2,0:T(8,128)S(1)}, s32[4]{0:T(128)}, /*index=5*/s32[]{:...) while((s32[]{:T(128)}, f32[3,512]{1,0:T(4,128)S(1)}, ...), condition=%wide.region_8.9_spmd.clone, body=%wide.region_3.8_spmd.clone.sunk | while | flops 424874496 | bytes 22858608 | solution.py:154
  123.9 7.8 %conditional.6 = ((f32[3,512]{1,0:T(4,128)S(1)}, f32[3,512]{1,0:T(4,128)S(1)}, f32[3,512,64]{1,2,0:T(8,128)S(1)})) conditional(s32[]{:T(128)} %convert_element_type.207, (f32[3,512]{1,0:T(4,128)S(1)}, f32[3,512]{1,0:T(4,128)S(1)}, f32[3,512,64]{1,2,0:T(8,128)S(1)}) %tuple.156, (s32[]{:T(128)}, s32[]{:T(128)}, s32[512]{0:T(512)}, ...), branch_computations={%region_4.4_spmd, %region_5.7_spmd} | conditional | flops 424874496 | bytes 22856236 | solution.py:150
  128.8 3.0 fusion.10
  145.1 37.2 %while.40 = (s32[]{:T(128)}, f32[512,3,64]{0,2,1:T(8,128)S(1)}, f32[4,1024,384]{2,1,0:T(8,128)}, s32[4]{0:T(128)S(1)}, s32[]{:T(128)}, /*index=5*/s32[]{:T(128)}...) while((s32[]{:T(128)}, f32[512,3,64]{0,2,1:T(8,128)S(1)}, ...), condition=%wide.region_14.15_spmd.clone, body=%wide.region_11.14_spmd.clone.sunk | while | flops 1024722432 | bytes 56325616 | solution.py:247
  147.8 8.3 %conditional.7 = (f32[512,3,64]{0,2,1:T(8,128)S(1)}, f32[1,1024,384]{1,2,0:T(8,128)S(1)}) conditional(s32[]{:T(128)} %convert_element_type.208, f32[512,3,64]{0,2,1:T(8,128)S(1)} %get-tuple-element.1217, (s32[]{:T(128)}, s32[]{:T(128)}, s32[512]{0:T(512)}, bf16[4,1024,3,64]{1,3,2,0:T(8,128)(2,1)S(1)}, s32[]{:T(128)}, ...), branch_computations={%region_12.12_spmd, %region_13.13_spmd} | conditional | flops 1024722432 | bytes 37448308 | solution.py:245
  149.4 3.3 fusion.23
  157.7 2.8 constant_dynamic-update-slice_fusion.2
  165.0 2.8 constant_dynamic-update-slice_fusion.2
  172.3 2.8 constant_dynamic-update-slice_fusion.2
  179.5 2.8 constant_dynamic-update-slice_fusion.2
  183.3 8.7 %all_gather.20 = bf16[512,768]{1,0:T(8,128)(2,1)S(1)} all-gather(bf16[128,768]{1,0:T(8,128)(2,1)S(1)} %copy-done.31), channel_id=1, replica_groups=mesh['ctx'=8,'tp'=4] {'tp'}, dimensions={0}, use_global_device_ids=true | all-gather | bytes 983040 | tf_op jit(solution)/shard_map/all_gather | solution.py:79
  192.0 4.2 fusion.44
  201.8 144.9 %reduce-scatter.7.cloned.1.call-done = f32[512,384]{1,0:T(8,128)} async-done(((f32[4096,384]{1,0:T(8,128)}), f32[512,384]{1,0:T(8,128)}) %reduce-scatter.7.cloned.1.call-update) | async-done | bytes 786448 | tf_op jit(solution)/shard_map/reduce_scatter | solution.py:249
  361.0 3.3 fusion.91
  371.1 20.6 %all-reduce.1 = (f32[2,192]{1,0:T(2,128)}, f32[768]{0:T(1024)}) all-reduce(f32[2,192]{1,0:T(2,128)S(1)} %pad_maximum_fusion.4, f32[768]{0:T(1024)S(1)} %get-tuple-element.970), channel_id=1, replica_groups=mesh['ctx'=8,'tp'=4] {'ctx'}, use_global_device_ids=true, to_apply=%region_33.34 | all-reduce | flops 1152 | bytes 9216 | tf_op jit(solution)/shard_map/psum | solution.py:284
  391.7 15.1 %reduce-scatter.9.cloned.1.call-done = f32[128,768]{1,0:T(8,128)} async-done(((f32[512,768]{1,0:T(8,128)}), f32[128,768]{1,0:T(8,128)}) %reduce-scatter.9.cloned.1.call-update) | async-done | bytes 393232 | tf_op jit(solution)/shard_map/reduce_scatter | solution.py:269
  408.3 28.8 %reduce-scatter.5.cloned.1.call-done = f32[128,768]{1,0:T(8,128)} async-done(((f32[512,768]{1,0:T(8,128)}), f32[128,768]{1,0:T(8,128)}) %reduce-scatter.5.cloned.1.call-update) | async-done | bytes 393232 | tf_op jit(solution)/shard_map/reduce_scatter | solution.py:165
  439.5 43.0 %all-reduce = (f32[768]{0:T(1024)}, f32[768]{0:T(1024)}, f32[768]{0:T(1024)}, f32[768]{0:T(1024)}, f32[768]{0:T(1024)S(1)}) all-reduce(f32[768]{0:T(1024)S(1)} %get-tuple-element.862, f32[768]{0:T(1024)S(1)} %get-tuple-element.867, f32[768]{0:T(1024)S(1)} %get-tuple-element.871, ...), channel_id=1, replica_groups=mesh['ctx'=8,'tp'=4] {'ctx','tp'}, use_global_device_ids=true, to_apply=%region_23.24 | all-reduce | flops 3840 | bytes 30720 | tf_op jit(solution)/shard_map/psum | solution.py:274
  482.5 193.0 %all-reduce.5.cloned.1.call-done = (f32[768,3,192]{0,2,1:T(8,128)}, f32[192,768]{1,0:T(8,128)}, f32[768,768]{1,0:T(8,128)}, f32[768,768]{1,0:T(8,128)}) async-done(((f32[768,3,192]{0,2,1:T(8,128)}, f32[192,768]{1,0:T(8,128)}, f32[768,768]{1,0:T(8,128)}, f32[768,768]{1,0:T(8,128)}), (f32[768,3,192]{0,2,1:T(8,128)}, f32[192,768]{1,0:T(8,128)}, f32[768,768]{1,0:T(8,128)}, ...) | async-done | bytes 7077904 | tf_op jit(solution)/shard_map/psum | solution.py:284
  676.0 2.9 copy.118
  (245 shorter events, 82.0 us)
Async XLA Ops:
  7.2 184.8 %copy-start = (bf16[768,768]{1,0:T(8,128)(2,1)S(1)}, bf16[768,768]{1,0:T(8,128)(2,1)}, u32[]{:S(2)}) copy-start(bf16[768,768]{1,0:T(8,128)(2,1)} %param.33) | copy-start | bytes 3538948
  7.2 14.4 %copy-start.12 = (bf16[768,3,192]{0,2,1:T(8,128)(2,1)S(1)}, bf16[768,3,192]{0,2,1:T(8,128)(2,1)}, u32[]{:S(2)}) copy-start(bf16[768,3,192]{0,2,1:T(8,128)(2,1)} %param.29) | copy-start | bytes 2654212
  7.2 64.4 %all-gather.3.cloned.1.call-start = ((), (), s32[]{:S(2)}) async-start(), calls=%async_computation.4 | async-start | bytes 1769472 | tf_op jit(solution)/shard_map/all_gather | solution.py:131
  8.5 13.1 %copy-start.41 = (f32[128]{0:T(128)}, f32[128]{0:T(128)S(1)}, u32[]{:S(2)}) copy-start(f32[128]{0:T(128)S(1)} %broadcast_multiply_fusion.5) | copy-start | bytes 1540
  9.6 12.0 %copy-start.44 = (f32[128]{0:T(128)}, f32[128]{0:T(128)S(1)}, u32[]{:S(2)}) copy-start(f32[128]{0:T(128)S(1)} %add_rsqrt_fusion) | copy-start | bytes 1540
  24.8 12.5 %copy-start.23 = (bf16[192,768]{1,0:T(8,128)(2,1)S(1)}, bf16[192,768]{1,0:T(8,128)(2,1)}, u32[]{:S(2)}) copy-start(bf16[192,768]{1,0:T(8,128)(2,1)} %param.31) | copy-start | bytes 884740
  25.5 12.2 %copy-start.34 = (f32[512,16]{0,1:T(8,128)}, f32[512,16]{0,1:T(8,128)S(1)}, u32[]{:S(2)}) copy-start(f32[512,16]{0,1:T(8,128)S(1)} %get-tuple-element.966) | copy-start | bytes 98308
  26.2 90.6 %all-gather.5.cloned.1.call-start = ((), (), s32[]{:S(2)}) async-start(), calls=%async_computation.5 | async-start | bytes 1769472 | tf_op jit(solution)/shard_map/all_gather | solution.py:132
  27.0 319.7 %reduce-scatter.7.cloned.1.call-start = ((), (), s32[]{:S(2)}) async-start(), calls=%async_computation.7 | async-start | bytes 7077888 | tf_op jit(solution)/shard_map/reduce_scatter | solution.py:249
  182.3 9.7 %copy-start.51 = (f32[768]{0:T(1024)S(1)}, f32[768]{0:T(1024)}, u32[]{:S(2)}) copy-start(f32[768]{0:T(1024)} %param.34) | copy-start | bytes 9220
  182.4 209.3 %reduce-scatter.11.cloned.1.call-start = ((), (), s32[]{:S(2)}) async-start(), calls=%async_computation.9 | async-start | bytes 1966080 | tf_op jit(solution)/shard_map/reduce_scatter | solution.py:270
  192.0 4.3 copy-start.21
  200.3 206.5 %reduce-scatter.9.cloned.1.call-start = ((), (), s32[]{:S(2)}) async-start(), calls=%async_computation.8 | async-start | bytes 1966080 | tf_op jit(solution)/shard_map/reduce_scatter | solution.py:269
  356.5 80.7 %reduce-scatter.5.cloned.1.call-start = ((), (), s32[]{:S(2)}) async-start(), calls=%async_computation.6 | async-start | bytes 1966080 | tf_op jit(solution)/shard_map/reduce_scatter | solution.py:165
  359.9 315.5 %all-reduce.5.cloned.1.call-start = ((), (), s32[]{:S(2)}) async-start(), calls=%async_computation.10 | async-start | bytes 14155776 | tf_op jit(solution)/shard_map/psum | solution.py:284
  369.9 36.9 %copy-start.11 = (bf16[128,768]{1,0:T(8,128)(2,1)S(1)}, bf16[128,768]{1,0:T(8,128)(2,1)}, u32[]{:S(2)}) copy-start(bf16[128,768]{1,0:T(8,128)(2,1)} %param.23) | copy-start | bytes 589828
  369.9 36.9 %copy-start.38 = (f32[768]{0:T(1024)S(1)}, f32[768]{0:T(1024)}, u32[]{:S(2)}) copy-start(f32[768]{0:T(1024)} %param.27) | copy-start | bytes 9220
  369.9 36.9 %copy-start.39 = (f32[768]{0:T(1024)S(1)}, f32[768]{0:T(1024)}, u32[]{:S(2)}) copy-start(f32[768]{0:T(1024)} %param.25) | copy-start | bytes 9220
  369.9 36.9 %copy-start.42 = (f32[128]{0:T(128)S(1)}, f32[128]{0:T(128)}, u32[]{:S(2)}) copy-start(f32[128]{0:T(128)} %copy-done.41) | copy-start | bytes 1540
  369.9 36.9 %copy-start.45 = (f32[128]{0:T(128)S(1)}, f32[128]{0:T(128)}, u32[]{:S(2)}) copy-start(f32[128]{0:T(128)} %copy-done.44) | copy-start | bytes 1540
  369.9 67.2 %copy-start.46 = (f32[768]{0:T(1024)S(1)}, f32[768]{0:T(1024)}, u32[]{:S(2)}) copy-start(f32[768]{0:T(1024)} %param.36) | copy-start | bytes 9220
  369.9 67.2 %copy-start.47 = (f32[768]{0:T(1024)S(1)}, f32[768]{0:T(1024)}, u32[]{:S(2)}) copy-start(f32[768]{0:T(1024)} %param.32) | copy-start | bytes 9220
  370.9 66.3 %copy-start.30 = (bf16[128,768]{1,0:T(8,128)(2,1)S(1)}, bf16[128,768]{1,0:T(8,128)(2,1)}, u32[]{:S(2)}) copy-start(bf16[128,768]{1,0:T(8,128)(2,1)} %param.37) | copy-start | bytes 589828
  482.5 196.5 %copy-start.48 = (f32[768]{0:T(1024)}, f32[768]{0:T(1024)S(1)}, u32[]{:S(2)}) copy-start(f32[768]{0:T(1024)S(1)} %get-tuple-element.1287) | copy-start | bytes 9220
  (41 other events, 81.0 us)
Sparse Core Ops, SparseCore 0:
  26.3 45.2 all-gather.2
  74.2 42.5 all-gather.4
  182.5 164.1 reduce-scatter.6
  349.1 27.2 reduce-scatter.10
  378.7 27.9 reduce-scatter.8
  409.2 27.9 reduce-scatter.4
  442.7 232.6 all-reduce.4
where the time goes:
time: 692 us; the launch traced here: 691 us
  waiting for transfers between devices  460 us (66%)
  blocking collectives  91.1 us (13%)
  local copies, waits for them, and re-layouts  54.8 us (8%)
  matrix products  33.3 us (5%)
  other arithmetic  20.3 us (3%)
  loops' own time  16 us (2%)
  between operations  14.7 us (2%)
    psum x1, waiting for transfers between devices, local(): lax.psum((grad_qkv, qv_bias_grad, grad_dense, grad_up, grad_up_bias, grad...  193 us
    reduce_scatter x1, waiting for transfers between devices, local(): lax.psum_scatter(key_terms, 'ctx', scatter_dimension=0, tiled=True)  145 us
    all_gather x1, waiting for transfers between devices, local(): value_rows = lax.all_gather(values, 'ctx', axis=0, tiled=True)  43.7 us
    psum x1, blocking collectives, local(): lax.psum((jnp.sum(own_attn * hat_one, axis=0), jnp.sum(own_attn, axis=0),...  43 us
    all_gather x1, waiting for transfers between devices, local(): key_rows = lax.all_gather(keys_rot, 'ctx', axis=0, tiled=True)  33.9 us
    reduce_scatter x1, waiting for transfers between devices, local(): lax.psum_scatter(attn_part + mlp_part, 'tp', scatter_dimension=0, tiled=T...  28.8 us
    psum x1, blocking collectives, local(): lax.psum((grad_qkv, qv_bias_grad, grad_dense, grad_up, grad_up_bias, grad...  20.6 us
    dynamic_update_slice x8, local copies, waits for them, and re-layouts, local(): query_grad, key_terms = lax.scan(back_step, zero_query, back_inputs)  17.6 us
  transfers between devices with their start and end apart: 7, of which 6 were waited for; matrix products, arithmetic and copies ran while one was open for 5% of the time, Pallas kernels for 0%

commit v1 on v0

--- a/solution.py
+++ b/solution.py
@@ -8,6 +8,11 @@
 HD = 64
 ROT = 16
 norm_eps = 1e-05
+process_weights = lambda v0, mine, ax_name: jnp.split(
+    jax.lax.all_gather(jnp.concatenate([v0, mine], 1), ax_name, axis=0, tiled=True),
+    [v0.shape[1]],
+    axis=1,
+)
 
 
 def layer_norm(values, scale, shift):
@@ -128,8 +133,7 @@
         jnp.zeros((head_count, block_rows, HD), jnp.float32),
     )
     running = initial
-    key_rows = lax.all_gather(keys_rot, "ctx", axis=0, tiled=True)
-    value_rows = lax.all_gather(values, "ctx", axis=0, tiled=True)
+    key_rows, value_rows = process_weights(keys_rot, values, "ctx")
     length = key_rows.shape[0]
     attend_step_rows = block_length(length)
     steps_count = length // attend_step_rows

time: 692 us -> 754 us (1.090)
  waiting for transfers between devices: 460 us -> 521 us
    all_gather x2 -> x3, waiting for transfers between devices: 77.6 us -> 136 us  [the longest x1 60.8 us: jax.lax.all_gather(jnp.concatenate([v0, mine], 1), ax_name, axis=0, tiled...]
    unnamed x99 -> x89, local copies, waits for them, and re-layouts: 15.8 us -> 14.7 us
  transfers between devices with their start and end apart: 7 -> 8, of which waited for: 6 -> 7; matrix products, arithmetic and copies ran while one was open for 5% -> 5% of each run, Pallas kernels for 0% -> 0%
where the time goes in v1:
time: 754 us; the launch traced here: 752 us
  waiting for transfers between devices  521 us (69%)
  blocking collectives  91.2 us (12%)
  local copies, waits for them, and re-layouts  50.5 us (7%)
  matrix products  36.6 us (5%)
  other arithmetic  21.9 us (3%)
  loops' own time  16.4 us (2%)
  between operations  14.6 us (2%)
    psum x1, waiting for transfers between devices, local(): lax.psum((grad_qkv, qv_bias_grad, grad_dense, grad_up, grad_up_bias, grad...  193 us
    reduce_scatter x1, waiting for transfers between devices, local(): lax.psum_scatter(key_terms, 'ctx', scatter_dimension=0, tiled=True)  147 us
    all_gather x1, waiting for transfers between devices, jax.lax.all_gather(jnp.concatenate([v0, mine], 1), ax_name, axis=0, tiled...  60.8 us
    psum x1, blocking collectives, local(): lax.psum((jnp.sum(own_attn * hat_one, axis=0), jnp.sum(own_attn, axis=0),...  43 us
    all_gather x1, waiting for transfers between devices, local(): lax.all_gather(values, 'ctx', axis=0, tiled=True)  42.5 us
    all_gather x1, waiting for transfers between devices, local(): lax.all_gather(keys_rot, 'ctx', axis=0, tiled=True)  32.3 us
    reduce_scatter x1, waiting for transfers between devices, local(): lax.psum_scatter(attn_part + mlp_part, 'tp', scatter_dimension=0, tiled=T...  29 us
    psum x1, blocking collectives, local(): lax.psum((grad_qkv, qv_bias_grad, grad_dense, grad_up, grad_up_bias, grad...  20.8 us
  transfers between devices with their start and end apart: 8, of which 7 were waited for; matrix products, arithmetic and copies ran while one was open for 5% of the time, Pallas kernels for 0%

profile of v1, /device:TPU:0, one launch (start us, length us, event | category | flops | bytes accessed | tf_op | source)
XLA Modules:
  0.0 752.2 jit_solution(12467034180665352706)
XLA Ops:
  11.9 10.1 %all_gather.18 = bf16[512,768]{1,0:T(8,128)(2,1)S(1)} all-gather(bf16[128,768]{1,0:T(8,128)(2,1)S(1)} %get-tuple-element.960), channel_id=1, replica_groups=mesh['ctx'=8,'tp'=4] {'tp'}, dimensions={0}, use_global_device_ids=true | all-gather | bytes 983040 | tf_op jit(solution)/shard_map/all_gather | solution.py:83
  28.4 8.7 %all_gather.23 = bf16[512,768]{1,0:T(8,128)(2,1)S(1)} all-gather(bf16[128,768]{1,0:T(8,128)(2,1)S(1)} %copy-done.24), channel_id=1, replica_groups=mesh['ctx'=8,'tp'=4] {'tp'}, dimensions={0}, use_global_device_ids=true | all-gather | bytes 983040 | tf_op jit(solution)/shard_map/all_gather | solution.py:173
  39.1 32.3 %all-gather.6.cloned.1.call-done = bf16[4096,3,64]{0,2,1:T(8,128)(2,1)} async-done(((bf16[512,3,64]{0,2,1:T(8,128)(2,1)}), bf16[4096,3,64]{0,2,1:T(8,128)(2,1)}) %all-gather.6.cloned.1.call-update) | async-done | bytes 1572880 | tf_op jit(solution)/shard_map/all_gather | solution.py:201
  71.4 2.7 copy.79
  74.1 42.5 %all-gather.8.cloned.1.call-done = bf16[4096,3,64]{0,2,1:T(8,128)(2,1)} async-done(((bf16[512,3,64]{0,2,1:T(8,128)(2,1)}), bf16[4096,3,64]{0,2,1:T(8,128)(2,1)}) %all-gather.8.cloned.1.call-update) | async-done | bytes 1572880 | tf_op jit(solution)/shard_map/all_gather | solution.py:202
  116.7 2.7 copy.78
  119.4 60.8 %all-gather.4.cloned.1.call-done = bf16[4096,6,64]{0,2,1:T(8,128)(2,1)} async-done(((bf16[512,6,64]{0,2,1:T(8,128)(2,1)}), bf16[4096,6,64]{0,2,1:T(8,128)(2,1)}) %all-gather.4.cloned.1.call-update) | async-done | bytes 3145744 | tf_op jit(solution)/shard_map/all_gather | solution.py:12
  183.9 17.0 %while.39 = (s32[]{:T(128)}, f32[3,512]{1,0:T(4,128)S(1)}, f32[3,512]{1,0:T(4,128)S(1)}, f32[3,512,64]{1,2,0:T(8,128)S(1)}, s32[4]{0:T(128)S(1)}, /*index=5*/s32...) while((s32[]{:T(128)}, f32[3,512]{1,0:T(4,128)S(1)}, ...), condition=%wide.region_8.9_spmd.clone, body=%wide.region_3.8_spmd.clone.sunk | while | flops 424874496 | bytes 22858608 | solution.py:158
  186.6 6.5 conditional.6
  190.2 3.0 fusion.10
  203.2 38.5 %while.40 = (s32[]{:T(128)}, f32[512,3,64]{0,2,1:T(8,128)S(1)}, f32[4,1024,384]{2,1,0:T(8,128)}, s32[4]{0:T(128)S(1)}, s32[]{:T(128)}, /*index=5*/s32[]{:T(128)}...) while((s32[]{:T(128)}, f32[512,3,64]{0,2,1:T(8,128)S(1)}, ...), condition=%wide.region_14.15_spmd.clone, body=%wide.region_11.14_spmd.clone.sunk | while | flops 1024722432 | bytes 44522088 | solution.py:251
  205.8 10.4 %conditional.7 = (f32[512,3,64]{0,2,1:T(8,128)S(1)}, f32[1,1024,384]{1,2,0:T(8,128)S(1)}) conditional(s32[]{:T(128)} %convert_element_type.208, f32[512,3,64]{0,2,1:T(8,128)S(1)} %get-tuple-element.1219, (s32[]{:T(128)}, s32[]{:T(128)}, s32[512]{0:T(512)S(1)}, bf16[4,1024,3,64]{1,3,2,0:T(8,128)(2,1)}, s32[]{:T(128)}, ...), branch_computations={%region_12.12_spmd, %region_13.13_spmd} | conditional | flops 1024722432 | bytes 38227564 | solution.py:249
  208.4 3.3 fusion.23
  217.8 2.7 constant_dynamic-update-slice_fusion.2
  242.6 8.6 %all_gather.20 = bf16[512,768]{1,0:T(8,128)(2,1)S(1)} all-gather(bf16[128,768]{1,0:T(8,128)(2,1)S(1)} %copy-done.26), channel_id=1, replica_groups=mesh['ctx'=8,'tp'=4] {'tp'}, dimensions={0}, use_global_device_ids=true | all-gather | bytes 983040 | tf_op jit(solution)/shard_map/all_gather | solution.py:84
  251.3 4.5 fusion.44
  261.3 146.8 %reduce-scatter.7.cloned.1.call-done = f32[512,384]{1,0:T(8,128)} async-done(((f32[4096,384]{1,0:T(8,128)}), f32[512,384]{1,0:T(8,128)}) %reduce-scatter.7.cloned.1.call-update) | async-done | bytes 786448 | tf_op jit(solution)/shard_map/reduce_scatter | solution.py:253
  421.8 3.6 fusion.91
  432.1 20.8 %all-reduce.1 = (f32[2,192]{1,0:T(2,128)}, f32[768]{0:T(1024)}) all-reduce(f32[2,192]{1,0:T(2,128)S(1)} %pad_maximum_fusion.5, f32[768]{0:T(1024)S(1)} %get-tuple-element.972), channel_id=1, replica_groups=mesh['ctx'=8,'tp'=4] {'ctx'}, use_global_device_ids=true, to_apply=%region_33.34 | all-reduce | flops 1152 | bytes 9216 | tf_op jit(solution)/shard_map/psum | solution.py:288
  452.8 15.4 %reduce-scatter.9.cloned.1.call-done = f32[128,768]{1,0:T(8,128)} async-done(((f32[512,768]{1,0:T(8,128)}), f32[128,768]{1,0:T(8,128)}) %reduce-scatter.9.cloned.1.call-update) | async-done | bytes 393232 | tf_op jit(solution)/shard_map/reduce_scatter | solution.py:273
  469.8 29.0 %reduce-scatter.5.cloned.1.call-done = f32[128,768]{1,0:T(8,128)} async-done(((f32[512,768]{1,0:T(8,128)}), f32[128,768]{1,0:T(8,128)}) %reduce-scatter.5.cloned.1.call-update) | async-done | bytes 393232 | tf_op jit(solution)/shard_map/reduce_scatter | solution.py:169
  501.1 43.0 %all-reduce = (f32[768]{0:T(1024)}, f32[768]{0:T(1024)}, f32[768]{0:T(1024)}, f32[768]{0:T(1024)}, f32[768]{0:T(1024)S(1)}) all-reduce(f32[768]{0:T(1024)S(1)} %get-tuple-element.862, f32[768]{0:T(1024)S(1)} %get-tuple-element.867, f32[768]{0:T(1024)S(1)} %get-tuple-element.871, ...), channel_id=1, replica_groups=mesh['ctx'=8,'tp'=4] {'ctx','tp'}, use_global_device_ids=true, to_apply=%region_23.24 | all-reduce | flops 3840 | bytes 30720 | tf_op jit(solution)/shard_map/psum | solution.py:278
  544.1 192.9 %all-reduce.5.cloned.1.call-done = (f32[768,3,192]{0,2,1:T(8,128)}, f32[192,768]{1,0:T(8,128)}, f32[768,768]{1,0:T(8,128)}, f32[768,768]{1,0:T(8,128)}) async-done(((f32[768,3,192]{0,2,1:T(8,128)}, f32[192,768]{1,0:T(8,128)}, f32[768,768]{1,0:T(8,128)}, f32[768,768]{1,0:T(8,128)}), (f32[768,3,192]{0,2,1:T(8,128)}, f32[192,768]{1,0:T(8,128)}, f32[768,768]{1,0:T(8,128)}, ...) | async-done | bytes 7077904 | tf_op jit(solution)/shard_map/psum | solution.py:288
  737.7 2.9 copy.124
  (242 shorter events, 85.4 us)
Async XLA Ops:
  7.2 244.1 %copy-start = (bf16[768,768]{1,0:T(8,128)(2,1)S(1)}, bf16[768,768]{1,0:T(8,128)(2,1)}, u32[]{:S(2)}) copy-start(bf16[768,768]{1,0:T(8,128)(2,1)} %param.33) | copy-start | bytes 3538948
  7.2 14.8 %copy-start.9 = (bf16[768,3,192]{0,2,1:T(8,128)(2,1)S(1)}, bf16[768,3,192]{0,2,1:T(8,128)(2,1)}, u32[]{:S(2)}) copy-start(bf16[768,3,192]{0,2,1:T(8,128)(2,1)} %param.29) | copy-start | bytes 2654212
  7.2 64.2 %all-gather.6.cloned.1.call-start = ((), (), s32[]{:S(2)}) async-start(), calls=%async_computation.6 | async-start | bytes 1769472 | tf_op jit(solution)/shard_map/all_gather | solution.py:201
  10.0 12.6 %copy-start.36 = (f32[128]{0:T(128)}, f32[128]{0:T(128)S(1)}, u32[]{:S(2)}) copy-start(f32[128]{0:T(128)S(1)} %add_rsqrt_fusion) | copy-start | bytes 1540
  26.0 11.9 %copy-start.18 = (bf16[192,768]{1,0:T(8,128)(2,1)S(1)}, bf16[192,768]{1,0:T(8,128)(2,1)}, u32[]{:S(2)}) copy-start(bf16[192,768]{1,0:T(8,128)(2,1)} %param.31) | copy-start | bytes 884740
  26.0 90.6 %all-gather.8.cloned.1.call-start = ((), (), s32[]{:S(2)}) async-start(), calls=%async_computation.7 | async-start | bytes 1769472 | tf_op jit(solution)/shard_map/all_gather | solution.py:202
  26.8 153.4 %all-gather.4.cloned.1.call-start = ((), (), s32[]{:S(2)}) async-start(), calls=%async_computation.4 | async-start | bytes 3538944 | tf_op jit(solution)/shard_map/all_gather | solution.py:12
  27.6 380.5 %reduce-scatter.7.cloned.1.call-start = ((), (), s32[]{:S(2)}) async-start(), calls=%async_computation.8 | async-start | bytes 7077888 | tf_op jit(solution)/shard_map/reduce_scatter | solution.py:253
  241.7 9.5 %copy-start.44 = (f32[768]{0:T(1024)S(1)}, f32[768]{0:T(1024)}, u32[]{:S(2)}) copy-start(f32[768]{0:T(1024)} %param.34) | copy-start | bytes 9220
  241.7 211.1 %reduce-scatter.11.cloned.1.call-start = ((), (), s32[]{:S(2)}) async-start(), calls=%async_computation.10 | async-start | bytes 1966080 | tf_op jit(solution)/shard_map/reduce_scatter | solution.py:274
  251.2 4.5 copy-start.2
  251.3 4.5 copy-start.16
  259.8 208.4 %reduce-scatter.9.cloned.1.call-start = ((), (), s32[]{:S(2)}) async-start(), calls=%async_computation.9 | async-start | bytes 1966080 | tf_op jit(solution)/shard_map/reduce_scatter | solution.py:273
  260.6 151.7 %copy-start.20 = (f32[512,3,16]{0,2,1:T(8,128)}, f32[512,3,16]{0,2,1:T(8,128)S(1)}, u32[]{:S(2)}) copy-start(f32[512,3,16]{0,2,1:T(8,128)S(1)} %fusion.102) | copy-start | bytes 294916
  418.4 80.4 %reduce-scatter.5.cloned.1.call-start = ((), (), s32[]{:S(2)}) async-start(), calls=%async_computation.5 | async-start | bytes 1966080 | tf_op jit(solution)/shard_map/reduce_scatter | solution.py:169
  421.7 315.3 %all-reduce.5.cloned.1.call-start = ((), (), s32[]{:S(2)}) async-start(), calls=%async_computation.11 | async-start | bytes 14155776 | tf_op jit(solution)/shard_map/psum | solution.py:288
  430.9 37.4 %copy-start.8 = (bf16[128,768]{1,0:T(8,128)(2,1)S(1)}, bf16[128,768]{1,0:T(8,128)(2,1)}, u32[]{:S(2)}) copy-start(bf16[128,768]{1,0:T(8,128)(2,1)} %param.23) | copy-start | bytes 589828
  430.9 37.4 %copy-start.32 = (f32[768]{0:T(1024)S(1)}, f32[768]{0:T(1024)}, u32[]{:S(2)}) copy-start(f32[768]{0:T(1024)} %param.27) | copy-start | bytes 9220
  430.9 37.4 %copy-start.33 = (f32[768]{0:T(1024)S(1)}, f32[768]{0:T(1024)}, u32[]{:S(2)}) copy-start(f32[768]{0:T(1024)} %param.25) | copy-start | bytes 9220
  430.9 37.3 %copy-start.37 = (f32[128]{0:T(128)S(1)}, f32[128]{0:T(128)}, u32[]{:S(2)}) copy-start(f32[128]{0:T(128)} %copy-done.36) | copy-start | bytes 1540
  430.9 67.9 %copy-start.38 = (f32[768]{0:T(1024)S(1)}, f32[768]{0:T(1024)}, u32[]{:S(2)}) copy-start(f32[768]{0:T(1024)} %param.36) | copy-start | bytes 9220
  430.9 67.9 %copy-start.39 = (f32[768]{0:T(1024)S(1)}, f32[768]{0:T(1024)}, u32[]{:S(2)}) copy-start(f32[768]{0:T(1024)} %param.32) | copy-start | bytes 9220
  431.9 66.9 %copy-start.25 = (bf16[128,768]{1,0:T(8,128)(2,1)S(1)}, bf16[128,768]{1,0:T(8,128)(2,1)}, u32[]{:S(2)}) copy-start(bf16[128,768]{1,0:T(8,128)(2,1)} %param.37) | copy-start | bytes 589828
  544.1 196.5 %copy-start.40 = (f32[768]{0:T(1024)}, f32[768]{0:T(1024)S(1)}, u32[]{:S(2)}) copy-start(f32[768]{0:T(1024)S(1)} %get-tuple-element.1289) | copy-start | bytes 9220
  (37 other events, 75.4 us)
Sparse Core Ops, SparseCore 0:
  26.1 45.2 all-gather.5
  74.0 42.5 all-gather.7
  119.3 60.8 all-gather.3
  241.8 166.2 reduce-scatter.6
  410.5 27.2 reduce-scatter.10
  440.2 27.9 reduce-scatter.8
  470.8 27.9 reduce-scatter.4
  504.4 232.6 all-reduce.4
